TPU v7x, 32 devices: a whole 2x2x4 slice. The times are simulated.
32 devices in a mesh: dp: 8 (over y, x, core), mp: 4 (over z).
Axes of the slice: x: 2, y: 2, z: 4, core: 2. Of those that a mesh axis runs over, the one named last changes fastest.
Arguments:
- frames: bfloat16 [16384, 640], P('dp'), may hold values from -6 to 6
- seg_ids: int32 [16384], P('dp'), may hold values from 0 to 15, as said below
- qkv_weight: bfloat16 [3, 640, 768], P(None, 'dp', 'mp'), may hold values from -0.25 to 0.25
- qkv_bias: float32 [2, 768], P(None, 'mp'), may hold values from -3 to 3
- out_weight: bfloat16 [768, 640], P('mp', 'dp'), may hold values from -1.5 to 1.5
- out_bias: float32 [640], replicated, may hold values from -3 to 3
- gain_one: float32 [640], replicated, may hold values from 0.1 to 1.9
- shift_one: float32 [640], replicated, may hold values from -3 to 3
- up_weight: bfloat16 [640, 2240], P('dp', 'mp'), may hold values from -0.25 to 0.25
- up_bias: float32 [2240], P('mp'), may hold values from -3 to 3
- down_weight: bfloat16 [2240, 640], P('mp', 'dp'), may hold values from -0.125 to 0.125
- down_bias: float32 [640], replicated, may hold values from -3 to 3
- gain_two: float32 [640], replicated, may hold values from 0.1 to 1.9
- shift_two: float32 [640], replicated, may hold values from -3 to 3
- cotangent: bfloat16 [16384, 640], P('dp'), may hold values from -6 to 6
Outputs:
- output_frames: bfloat16 [16384, 640], P(('dp', 'mp'))
- frames_grad: bfloat16 [16384, 640], P(('dp', 'mp'))
- qkv_grad: float32 [3, 640, 768], P(None, 'dp', 'mp')
- qkv_bias_grad: float32 [2, 768], P(None, 'mp')
- out_grad: float32 [768, 640], P('mp', 'dp')
- out_bias_grad: float32 [640], replicated
- gain_one_grad: float32 [640], replicated
- shift_one_grad: float32 [640], replicated
- up_grad: float32 [640, 2240], P('dp', 'mp')
- up_bias_grad: float32 [2240], P('mp')
- down_grad: float32 [2240, 640], P('mp', 'dp')
- down_bias_grad: float32 [640], replicated
- gain_two_grad: float32 [640], replicated
- shift_two_grad: float32 [640], replicated
Inputs may be any that keep to these rules, and one draw needn't show every extreme that they name: `seg_ids`: each block of 2048 frames that one index of dp holds contains 1 to 16 whole utterances laid end to end; within the block the number starts at 0 and rises by one at each new utterance. In every draw some block holds a single utterance of 2048 frames and some block holds 16 utterances.
All inputs are finite; a program needn't handle non-finite values.
Results may differ from a plain program's by a relative error of at most 0.019.
Values may be sent and summed in bfloat16 or wider, within the bound.
A program may use at most 192 MiB of HBM per device.

v0:
```python
import jax
import jax.numpy as jnp
from jax import lax
from jax.sharding import PartitionSpec as P

HEADS = 10
HD = 64
EPS = 1e-05
SCALE = 0.125


def cut_along(array, dim, length):
    before, after = (array.shape[:dim], array.shape[dim + 1 :])
    return jnp.moveaxis(array.reshape(*before, length, -1, *after), dim, 0)


def sum_at_owner(array, axis, dim):
    parts = cut_along(array, dim, lax.axis_size(axis))
    arrived = lax.all_to_all(parts, axis, split_axis=0, concat_axis=0, tiled=True)
    return arrived.astype(jnp.float32).sum(axis=0)


def norm_forward(summed):
    centre = summed - jnp.mean(summed, -1, keepdims=True)
    spread = jnp.mean(centre * centre, -1, keepdims=True)
    factor = lax.rsqrt(spread + EPS)
    return (centre * factor, factor)


def norm_backward(upper, normed, factor, gain):
    scaled = upper * gain
    return factor * (
        scaled
        - jnp.mean(scaled, -1, keepdims=True)
        - normed * jnp.mean(scaled * normed, -1, keepdims=True)
    )


def gelu_exact(values):
    return jax.nn.gelu(values, approximate=False)


def body(
    frames,
    seg_ids,
    qkv_weight,
    qkv_bias,
    out_weight,
    out_bias,
    gain_one,
    shift_one,
    up_weight,
    up_bias,
    down_weight,
    down_bias,
    gain_two,
    shift_two,
    cotangent,
):
    qkv_full, out_full, up_full, down_full = (
        lax.all_gather(qkv_weight, "dp", axis=1, tiled=True),
        lax.all_gather(out_weight, "dp", axis=1, tiled=True),
        lax.all_gather(up_weight, "dp", axis=0, tiled=True),
        lax.all_gather(down_weight, "dp", axis=1, tiled=True),
    )
    total_rows = frames.shape[0]
    mp_size = lax.axis_size("mp")
    mp_index = lax.axis_index("mp")
    share_rows = total_rows // mp_size
    share_start = mp_index * share_rows
    slot_count = qkv_weight.shape[2] // HD
    hidden_cols = up_weight.shape[1]
    live_count = HEADS // mp_size + (mp_index < HEADS % mp_size).astype(jnp.int32)
    live_mask = (jnp.arange(slot_count) < live_count).astype(jnp.float32)
    live_low = live_mask.astype(jnp.bfloat16)
    projected = jnp.einsum("rd,ids->irs", frames, qkv_full, preferred_element_type=jnp.float32)
    offsets = jnp.stack([qkv_bias[0], jnp.zeros_like(qkv_bias[0]), qkv_bias[1]])
    head_values = (
        (projected + offsets[:, None, :])
        .astype(jnp.bfloat16)
        .reshape(3, total_rows, slot_count, HD)
    )
    queries = head_values[0]
    keys_all = head_values[1]
    values = head_values[2]
    block_rows = min(512, total_rows)
    block_count = total_rows // block_rows

    def scores_at(anchor):
        query_block = lax.dynamic_slice_in_dim(queries, anchor, block_rows, 0)
        seg_block = lax.dynamic_slice_in_dim(seg_ids, anchor, block_rows, 0)
        raw_scores = (
            jnp.einsum("qhd,khd->hqk", query_block, keys_all, preferred_element_type=jnp.float32)
            * SCALE
        )
        same_utter = seg_block[:, None] == seg_ids[None, :]
        return (query_block, jnp.where(same_utter[None], raw_scores, -1e30))

    def attend(position):
        unused, scores = scores_at(position * block_rows)
        maxima = jnp.max(scores, -1, keepdims=True)
        raised = jnp.exp(scores - maxima)
        totals = jnp.sum(raised, -1, keepdims=True)
        prob_low = (raised / totals).astype(jnp.bfloat16)
        mixed = jnp.einsum("hqk,khd->qhd", prob_low, values, preferred_element_type=jnp.float32)
        return (mixed, maxima, totals)

    attended, all_maxima, all_totals = lax.map(attend, jnp.arange(block_count))
    attended = attended.reshape(total_rows, slot_count, HD) * live_mask[None, :, None]
    mixed_low = attended.reshape(total_rows, slot_count * HD).astype(jnp.bfloat16)
    frames_wide = frames.astype(jnp.float32)

    def share_of(array):
        return lax.dynamic_slice_in_dim(array, share_start, share_rows, 0)

    attention = lax.psum(
        jnp.dot(mixed_low, out_full, preferred_element_type=jnp.float32).astype(jnp.bfloat16), "mp"
    ).astype(jnp.float32)
    normed_one, factor_one = norm_forward(frames_wide + attention + out_bias)
    hidden = normed_one * gain_one + shift_one
    hidden_low = hidden.astype(jnp.bfloat16)
    act_low = gelu_exact(
        jnp.dot(hidden_low, up_full, preferred_element_type=jnp.float32) + up_bias
    ).astype(jnp.bfloat16)
    feed = lax.psum(
        jnp.dot(act_low, down_full, preferred_element_type=jnp.float32).astype(jnp.bfloat16), "mp"
    ).astype(jnp.float32)
    normed_two, factor_two = norm_forward(hidden + feed + down_bias)
    output_frames = share_of(normed_two * gain_two + shift_two).astype(jnp.bfloat16)
    upstream = cotangent.astype(jnp.float32)
    sum_two_grad = norm_backward(upstream, normed_two, factor_two, gain_two)
    sum_two_low = sum_two_grad.astype(jnp.bfloat16)
    pre_act = jnp.dot(hidden_low, up_full, preferred_element_type=jnp.float32) + up_bias
    activation, pullback = jax.vjp(gelu_exact, pre_act)
    act_low = activation.astype(jnp.bfloat16)
    grad_down = jnp.einsum("rf,rd->fd", act_low, sum_two_low, preferred_element_type=jnp.float32)
    act_grad = jnp.einsum("rd,fd->rf", sum_two_low, down_full, preferred_element_type=jnp.float32)
    pre_low = pullback(act_grad)[0].astype(jnp.bfloat16)
    grad_up = jnp.einsum("rd,rf->df", hidden_low, pre_low, preferred_element_type=jnp.float32)
    bias_up = jnp.sum(pre_low.astype(jnp.float32), 0)
    grad_up, bias_up, grad_down, pre_low = (grad_up, bias_up, grad_down, pre_low)
    hidden_part = jnp.einsum("rf,df->rd", pre_low, up_full, preferred_element_type=jnp.float32)
    hidden_grad = (
        lax.psum(hidden_part.astype(jnp.bfloat16), "mp").astype(jnp.float32) + sum_two_grad
    )
    sum_one_grad = norm_backward(hidden_grad, normed_one, factor_one, gain_one)
    sum_one_low = sum_one_grad.astype(jnp.bfloat16)
    grad_proj = jnp.einsum("rs,rd->sd", mixed_low, sum_one_low, preferred_element_type=jnp.float32)
    back_mixed = jnp.einsum("rd,sd->rs", sum_one_low, out_full, preferred_element_type=jnp.float32)
    back_mixed = (
        back_mixed.astype(jnp.bfloat16).reshape(total_rows, slot_count, HD)
        * live_low[None, :, None]
    )

    def step(running, record):
        key_grad, value_grad = running
        position, maxima, totals = record
        anchor = position * block_rows
        query_block, scores = scores_at(anchor)
        probs = jnp.exp(scores - maxima) / totals
        prob_low = probs.astype(jnp.bfloat16)
        back_block = lax.dynamic_slice_in_dim(back_mixed, anchor, block_rows, 0)
        value_grad = value_grad + jnp.einsum(
            "hqk,qhd->khd", prob_low, back_block, preferred_element_type=jnp.float32
        )
        prob_grad = jnp.einsum(
            "qhd,khd->hqk", back_block, values, preferred_element_type=jnp.float32
        )
        score_low = (probs * (prob_grad - jnp.sum(probs * prob_grad, -1, keepdims=True))).astype(
            jnp.bfloat16
        )
        query_grad = (
            jnp.einsum("hqk,khd->qhd", score_low, keys_all, preferred_element_type=jnp.float32)
            * SCALE
        )
        key_grad = (
            key_grad
            + jnp.einsum("hqk,qhd->khd", score_low, query_block, preferred_element_type=jnp.float32)
            * SCALE
        )
        return ((key_grad, value_grad), query_grad)

    zeros = jnp.zeros((total_rows, slot_count, HD), jnp.float32)
    (key_grad, value_grad), query_grad = lax.scan(
        step, (zeros, zeros), (jnp.arange(block_count), all_maxima, all_totals)
    )
    query_grad = query_grad.reshape(total_rows, slot_count, HD)
    grads_low = (
        jnp.stack([query_grad, key_grad, value_grad])
        .reshape(3, total_rows, slot_count * HD)
        .astype(jnp.bfloat16)
    )
    grad_qkv = jnp.einsum("rd,irs->ids", frames, grads_low, preferred_element_type=jnp.float32)
    bias_qkv = jnp.stack(
        [jnp.sum(grads_low[0].astype(jnp.float32), 0), jnp.sum(grads_low[2].astype(jnp.float32), 0)]
    )
    grad_qkv, bias_qkv, grad_proj, grads_low = (grad_qkv, bias_qkv, grad_proj, grads_low)
    input_part = jnp.einsum("irs,ids->rd", grads_low, qkv_full, preferred_element_type=jnp.float32)
    input_grad = lax.psum(input_part.astype(jnp.bfloat16), "mp").astype(jnp.float32) + sum_one_grad
    frames_grad = share_of(input_grad).astype(jnp.bfloat16)
    upstream_share = share_of(upstream)
    hidden_share = share_of(hidden_grad)
    out_bias_term = jnp.sum(share_of(sum_one_low).astype(jnp.float32), 0)
    gain_one_term = jnp.sum(hidden_share * share_of(normed_one), 0)
    shift_one_term = jnp.sum(hidden_share, 0)
    down_bias_term = jnp.sum(share_of(sum_two_low).astype(jnp.float32), 0)
    gain_two_term = jnp.sum(upstream_share * share_of(normed_two), 0)
    shift_two_term = jnp.sum(upstream_share, 0)
    matrix_grads = (
        sum_at_owner(grad_qkv.astype(jnp.bfloat16), "dp", 1),
        sum_at_owner(grad_proj.astype(jnp.bfloat16), "dp", 1),
        sum_at_owner(grad_up.astype(jnp.bfloat16), "dp", 0),
        sum_at_owner(grad_down.astype(jnp.bfloat16), "dp", 1),
    )
    slot_width = slot_count * HD
    padded_qkv = lax.dynamic_update_slice(
        jnp.zeros((2, mp_size * slot_width), jnp.float32), bias_qkv, (0, mp_index * slot_width)
    )
    padded_up = lax.dynamic_update_slice(
        jnp.zeros((mp_size * hidden_cols,), jnp.float32), bias_up, (mp_index * hidden_cols,)
    )
    summed = lax.psum(
        (
            padded_qkv,
            padded_up,
            out_bias_term,
            gain_one_term,
            shift_one_term,
            down_bias_term,
            gain_two_term,
            shift_two_term,
        ),
        ("dp", "mp"),
    )
    qkv_bias_grad = lax.dynamic_slice_in_dim(summed[0], mp_index * slot_width, slot_width, 1)
    up_bias_grad = lax.dynamic_slice_in_dim(summed[1], mp_index * hidden_cols, hidden_cols, 0)
    return (
        output_frames,
        frames_grad,
        matrix_grads[0],
        qkv_bias_grad,
        matrix_grads[1],
        summed[2],
        summed[3],
        summed[4],
        matrix_grads[2],
        up_bias_grad,
        matrix_grads[3],
        summed[5],
        summed[6],
        summed[7],
    )


def solution(mesh):
    in_specs = (
        P("dp", None),
        P("dp"),
        P(None, "dp", "mp"),
        P(None, "mp"),
        P("mp", "dp"),
        P(),
        P(),
        P(),
        P("dp", "mp"),
        P("mp"),
        P("mp", "dp"),
        P(),
        P(),
        P(),
        P("dp", None),
    )
    out_specs = (
        P(("dp", "mp"), None),
        P(("dp", "mp"), None),
        P(None, "dp", "mp"),
        P(None, "mp"),
        P("mp", "dp"),
        P(),
        P(),
        P(),
        P("dp", "mp"),
        P("mp"),
        P("mp", "dp"),
        P(),
        P(),
        P(),
    )
    return jax.shard_map(body, mesh=mesh, in_specs=in_specs, out_specs=out_specs, check_vma=False)
```

profile of v0, /device:TPU:0, one launch (start us, length us, event | category | flops | bytes accessed | tf_op | source)
XLA Modules:
  0.0 783.6 jit_solution(1316347857595142371)
XLA Ops:
  8.2 11.1 %all_gather.13 = bf16[192,640]{0,1:T(8,128)(2,1)S(1)} all-gather(bf16[192,80]{0,1:T(8,128)(2,1)} %param.23), channel_id=1, replica_groups=mesh['dp'=8,'mp'=4] {'dp'}, dimensions={1}, use_global_device_ids=true | all-gather | bytes 276480 | tf_op jit(solution)/shard_map/all_gather | solution.py:62
  19.3 10.8 %all_gather.12 = bf16[3,640,192]{2,1,0:T(8,128)(2,1)S(1)} all-gather(bf16[3,80,192]{2,1,0:T(8,128)(2,1)} %param.21), channel_id=1, replica_groups=mesh['dp'=8,'mp'=4] {'dp'}, dimensions={1}, use_global_device_ids=true | all-gather | bytes 829440 | tf_op jit(solution)/shard_map/all_gather | solution.py:61
  30.2 4.4 fusion.38
  35.3 124.3 %while.29 = (s32[]{:T(128)}, f32[4,512,3,64]{1,0,3,2:T(4,128)}, f32[4,3,512,1]{2,1,3,0:T(4,128)}, f32[4,3,512,1]{2,1,3,0:T(4,128)S(1)}, s32[4]{0:T(128)S(1)}, /*...) while((s32[]{:T(128)}, f32[4,512,3,64]{1,0,3,2:T(4,128)}, ...), condition=%wide.region_3.4_spmd, body=%wide.region_0.3_spmd.sunk | while | flops 844100608 | bytes 45756624 | solution.py:108
  37.3 6.0 fusion.104
  43.3 6.8 fusion.105
  50.1 6.7 fusion.106
  57.8 8.6 %dynamic_update_slice.30 = f32[4,512,3,64]{1,0,3,2:T(4,128)} dynamic-update-slice(f32[4,512,3,64]{1,0,3,2:T(4,128)} %get-tuple-element.413, f32[1,512,3,64]{1,0,3,2:T(1,128)S(1)} %copy.68, s32[]{:T(128)S(6)} %copy.77, s32[]{:T(128)} %constant.76.clone.1..sunk, s32[]{:T(128)} %constant.76.clone.1..sunk, s32[]{:T(128)} %constant.76.clone.1..sunk) | dynamic-update-slice | bytes 786436 | tf_op jit(solution)/shard_map/while/body/jit(dynamic_update_index_in_dim)/dynamic_update_slice | solution.py:108
  68.4 6.0 fusion.104
  74.4 6.8 fusion.105
  81.2 6.7 fusion.106
  88.9 8.6 %dynamic_update_slice.30 = f32[4,512,3,64]{1,0,3,2:T(4,128)} dynamic-update-slice(f32[4,512,3,64]{1,0,3,2:T(4,128)} %get-tuple-element.413, f32[1,512,3,64]{1,0,3,2:T(1,128)S(1)} %copy.68, s32[]{:T(128)S(6)} %copy.77, s32[]{:T(128)} %constant.76.clone.1..sunk, s32[]{:T(128)} %constant.76.clone.1..sunk, s32[]{:T(128)} %constant.76.clone.1..sunk) | dynamic-update-slice | bytes 786436 | tf_op jit(solution)/shard_map/while/body/jit(dynamic_update_index_in_dim)/dynamic_update_slice | solution.py:108
  99.5 6.0 fusion.104
  105.5 6.8 fusion.105
  112.3 6.7 fusion.106
  119.9 8.6 %dynamic_update_slice.30 = f32[4,512,3,64]{1,0,3,2:T(4,128)} dynamic-update-slice(f32[4,512,3,64]{1,0,3,2:T(4,128)} %get-tuple-element.413, f32[1,512,3,64]{1,0,3,2:T(1,128)S(1)} %copy.68, s32[]{:T(128)S(6)} %copy.77, s32[]{:T(128)} %constant.76.clone.1..sunk, s32[]{:T(128)} %constant.76.clone.1..sunk, s32[]{:T(128)} %constant.76.clone.1..sunk) | dynamic-update-slice | bytes 786436 | tf_op jit(solution)/shard_map/while/body/jit(dynamic_update_index_in_dim)/dynamic_update_slice | solution.py:108
  130.5 6.0 fusion.104
  136.6 6.8 fusion.105
  143.3 6.7 fusion.106
  151.0 8.6 %dynamic_update_slice.30 = f32[4,512,3,64]{1,0,3,2:T(4,128)} dynamic-update-slice(f32[4,512,3,64]{1,0,3,2:T(4,128)} %get-tuple-element.413, f32[1,512,3,64]{1,0,3,2:T(1,128)S(1)} %copy.68, s32[]{:T(128)S(6)} %copy.77, s32[]{:T(128)} %constant.76.clone.1..sunk, s32[]{:T(128)} %constant.76.clone.1..sunk, s32[]{:T(128)} %constant.76.clone.1..sunk) | dynamic-update-slice | bytes 786436 | tf_op jit(solution)/shard_map/while/body/jit(dynamic_update_index_in_dim)/dynamic_update_slice | solution.py:108
  166.6 11.7 %all_gather.14 = bf16[640,560]{1,0:T(8,128)(2,1)} all-gather(bf16[80,560]{1,0:T(8,128)(2,1)S(1)} %copy-done.29), channel_id=1, replica_groups=mesh['dp'=8,'mp'=4] {'dp'}, dimensions={0}, use_global_device_ids=true | all-gather | bytes 806400 | tf_op jit(solution)/shard_map/all_gather | solution.py:63
  178.3 11.1 %all_gather.15 = bf16[560,640]{0,1:T(8,128)(2,1)} all-gather(bf16[560,80]{0,1:T(8,128)(2,1)S(1)} %copy-done.30), channel_id=1, replica_groups=mesh['dp'=8,'mp'=4] {'dp'}, dimensions={1}, use_global_device_ids=true | all-gather | bytes 806400 | tf_op jit(solution)/shard_map/all_gather | solution.py:64
  189.4 81.7 %all-reduce.6.cloned.1.call-done = bf16[2048,640]{1,0:T(8,128)(2,1)} async-done(((bf16[2048,640]{1,0:T(8,128)(2,1)}), bf16[2048,640]{1,0:T(8,128)(2,1)}) %all-reduce.6.cloned.1.call-update) | async-done | bytes 2621456 | tf_op jit(solution)/shard_map/psum | solution.py:116
  277.4 13.3 %multiply_convert_fusion.1 = (bf16[2048,560]{0,1:T(8,128)(2,1)S(1)}, f32[2048,560]{0,1:T(8,128)}, f32[2048,560]{0,1:T(8,128)}) fusion(f32[560]{0:T(1024)S(1)} %copy-done.44, bf16[640,560]{1,0:T(8,128)(2,1)S(1)} %copy-done.23, f32[2048,640]{1,0:T(8,128)S(1)} %subtract_multiply_fusion.3, f32[640]{0:T(1024)S(1)} %copy-done.36, f32[640]{0:T(1024)S(1)} %copy-done.31), kind=kOutput, calls=%fused_computation.61 | convolution fusion | flops 1547632640 | bytes 17435840 | tf_op jit(solution)/shard_map/dot_general | solution.py:123
  296.3 103.0 %all-reduce.8.cloned.1.call-done = bf16[2048,640]{1,0:T(8,128)(2,1)} async-done(((bf16[2048,640]{1,0:T(8,128)(2,1)}), bf16[2048,640]{1,0:T(8,128)(2,1)}) %all-reduce.8.cloned.1.call-update) | async-done | bytes 2621456 | tf_op jit(solution)/shard_map/psum | solution.py:125
  399.3 4.5 fusion.52
  413.3 4.5 convert_reduce_fusion
  423.7 5.2 convolution_convert_fusion.5
  435.9 90.5 %all-reduce.10.cloned.1.call-done = bf16[2048,640]{1,0:T(8,128)(2,1)} async-done(((bf16[2048,640]{1,0:T(8,128)(2,1)}), bf16[2048,640]{1,0:T(8,128)(2,1)}) %all-reduce.10.cloned.1.call-update) | async-done | bytes 2621456 | tf_op jit(solution)/shard_map/psum | solution.py:144
  526.4 7.0 multiply_reduce_fusion.5
  533.5 6.6 fusion.57
  543.7 114.9 %while.30 = (s32[]{:T(128)}, f32[2048,3,64]{0,2,1:T(8,128)S(1)}, f32[2048,3,64]{0,2,1:T(8,128)S(1)}, bf16[4,512,3,64]{1,3,2,0:T(8,128)(2,1)}, s32[4]{0:T(128)S(1...) while((s32[]{:T(128)}, f32[2048,3,64]{0,2,1:T(8,128)S(1)}, ...), condition=%wide.region_17.18_spmd.clone, body=%wide.region_15.17_spmd.clone.sunk | while | flops 2047834624 | bytes 118950256 | solution.py:184
  549.6 7.7 multiply_reduce_fusion.10
  557.3 5.5 multiply_convert_fusion.6
  562.8 6.2 fusion.118
  578.3 7.7 multiply_reduce_fusion.10
  586.0 5.5 multiply_convert_fusion.6
  591.5 6.2 fusion.118
  607.1 7.7 multiply_reduce_fusion.10
  614.8 5.5 multiply_convert_fusion.6
  620.2 6.2 fusion.118
  635.8 7.7 multiply_reduce_fusion.10
  643.5 5.5 multiply_convert_fusion.6
  649.0 6.2 fusion.118
  670.3 4.5 convolution_convert_fusion.4
  687.8 5.0 all-to-all-done.2
  702.6 5.1 fusion.46
  721.3 44.5 %all-reduce = (f32[2,768]{1,0:T(2,128)S(1)}, f32[640]{0:T(1024)}, f32[640]{0:T(1024)}, f32[640]{0:T(1024)}, f32[2240]{0:T(1024)S(1)}, /*index=5*/f32[640]{0:T(1024)}, f32[640]{0:T(1024)}, f32[640]{0:T(1024)}) all-reduce(f32[2,768]{1,0:T(2,128)S(1)} %dynamic_update_slice.20, ...), channel_id=1, replica_groups=mesh['dp'=8,'mp'=4] {'dp','mp'}, use_global_device_ids=true, to_apply=%region_22.23 | all-reduce | flops 7616 | bytes 60928 | tf_op jit(solution)/shard_map/psum | solution.py:222
  (264 shorter events, 148.9 us)
Async XLA Ops:
  7.2 263.9 %all-reduce.6.cloned.1.call-start = ((), (), s32[]{:S(2)}) async-start(), calls=%async_computation.4 | async-start | bytes 5242880 | tf_op jit(solution)/shard_map/psum | solution.py:116
  7.4 155.2 %copy-start.39 = (f32[192]{0:T(256)}, f32[192]{0:T(256)S(1)}, u32[]{:S(2)}) copy-start(f32[192]{0:T(256)S(1)} %mul.192) | copy-start | bytes 2308
  30.1 4.6 copy-start.21
  159.6 6.8 copy-start.2
  159.6 6.8 copy-start.5
  159.6 6.8 copy-start.15
  159.6 6.9 copy-start.29
  162.6 15.7 %copy-start.30 = (bf16[560,80]{0,1:T(8,128)(2,1)S(1)}, bf16[560,80]{0,1:T(8,128)(2,1)}, u32[]{:S(2)}) copy-start(bf16[560,80]{0,1:T(8,128)(2,1)} %param.29) | copy-start | bytes 268804
  162.6 108.5 %copy-start.38 = (f32[640]{0:T(1024)S(1)}, f32[640]{0:T(1024)}, u32[]{:S(2)}) copy-start(f32[640]{0:T(1024)} %param.24) | copy-start | bytes 7684
  166.5 232.8 %all-reduce.8.cloned.1.call-start = ((), (), s32[]{:S(2)}) async-start(), calls=%async_computation.5 | async-start | bytes 5242880 | tf_op jit(solution)/shard_map/psum | solution.py:125
  166.5 108.1 %copy-start.11 = (bf16[2048,640]{1,0:T(8,128)(2,1)S(1)}, bf16[2048,640]{1,0:T(8,128)(2,1)}, u32[]{:S(2)}) copy-start(bf16[2048,640]{1,0:T(8,128)(2,1)} %param.19) | copy-start | bytes 7864324
  271.0 3.6 copy-start.12
  277.3 13.3 %copy-start = (f32[2048,640]{1,0:T(8,128)}, f32[2048,640]{1,0:T(8,128)S(1)}, u32[]{:S(2)}) copy-start(f32[2048,640]{1,0:T(8,128)S(1)} %subtract_multiply_fusion.3) | copy-start | bytes 15728644
  277.3 14.8 %copy-start.25 = (bf16[560,640]{0,1:T(8,128)(2,1)S(1)}, bf16[560,640]{0,1:T(8,128)(2,1)}, u32[]{:S(2)}) copy-start(bf16[560,640]{0,1:T(8,128)(2,1)} %all_gather.15) | copy-start | bytes 2150404
  292.1 107.2 %copy-start.35 = (f32[640]{0:T(1024)S(1)}, f32[640]{0:T(1024)}, u32[]{:S(2)}) copy-start(f32[640]{0:T(1024)} %param.30) | copy-start | bytes 7684
  296.0 230.4 %all-reduce.10.cloned.1.call-start = ((), (), s32[]{:S(2)}) async-start(), calls=%async_computation.6 | async-start | bytes 5242880 | tf_op jit(solution)/shard_map/psum | solution.py:144
  399.3 4.6 copy-start.10
  399.3 8.1 %slice-start = ((s8[5242880]{0:T(1024)(128)(4,1)}), s8[1048576]{0:T(1024)(128)(4,1)S(1)}, s32[]{:S(2)}) async-start(s8[5242880]{0:T(1024)(128)(4,1)} %bitcast.122), calls=%async_computation.8 | async-start | bytes 2097152
  403.9 3.6 copy-start.3
  403.9 3.6 copy-start.33
  403.9 4.5 slice-start.1
  403.9 9.3 %slice-start.2 = ((s8[4587520]{0:T(1024)(128)(4,1)}), s8[4194304]{0:T(1024)(128)(4,1)S(1)}, s32[]{:S(2)}) async-start(s8[4587520]{0:T(1024)(128)(4,1)} %bitcast.141), calls=%async_computation.10 | async-start | bytes 8388608
  403.9 9.3 %slice-start.4 = ((s8[4587520]{0:T(1024)(128)(4,1)}), s8[4194304]{0:T(1024)(128)(4,1)S(1)}, s32[]{:S(2)}) async-start(s8[4587520]{0:T(1024)(128)(4,1)} %bitcast.143), calls=%async_computation.12 | async-start | bytes 8388608
  408.4 4.8 slice-start.3
  408.4 4.8 slice-start.5
  413.2 4.6 copy-start.14
  413.2 5.9 copy-start.24
  431.2 244.8 %all-to-all-start.3 = ((bf16[8,560,80]{1,2,0:T(8,128)(2,1)}), bf16[8,560,80]{1,2,0:T(8,128)(2,1)}, u32[]{:S(2)}, u32[]{:S(2)}) async-start(bf16[8,560,80]{1,2,0:T(8,128)(2,1)} %bitcast.130), calls=%async_computation.3 | async-start | bytes 1638400 | tf_op jit(solution)/shard_map/all_to_all | solution.py:19
  435.4 339.0 %all-reduce.12.cloned.1.call-start = ((), (), s32[]{:S(2)}) async-start(), calls=%async_computation.7 | async-start | bytes 5242880 | tf_op jit(solution)/shard_map/psum | solution.py:199
  533.4 6.6 copy-start.9
  533.4 9.2 %copy-start.43 = (bf16[3]{0:T(256)(128)(2,1)S(1)}, bf16[3]{0:T(256)(128)(2,1)}, u32[]{:S(2)}) copy-start(bf16[3]{0:T(256)(128)(2,1)} %fusion.55) | copy-start | bytes 22
  562.8 6.2 copy-start.26
  591.5 6.2 copy-start.26
  620.2 6.2 copy-start.26
  649.0 6.2 copy-start.26
  666.2 4.0 copy-start.32
  666.2 4.0 copy-start.37
  666.2 4.1 copy-start.47
  674.8 5.1 copy-start.4
  676.0 6.5 copy-start.42
  676.0 6.8 copy-start.34
  676.0 6.8 copy-start.41
  676.0 16.8 %all-to-all-start.2 = ((bf16[8,80,560]{2,1,0:T(8,128)(2,1)}), bf16[8,80,560]{2,1,0:T(8,128)(2,1)S(1)}, u32[]{:S(2)}, u32[]{:S(2)}) async-start(bf16[8,80,560]{2,1,0:T(8,128)(2,1)} %bitcast.21), calls=%async_computation.2 | async-start | bytes 1638400 | tf_op jit(solution)/shard_map/all_to_all | solution.py:19
  682.5 11.1 %copy-start.8 = (bf16[2048,640]{1,0:T(8,128)(2,1)S(1)}, bf16[2048,640]{1,0:T(8,128)(2,1)}, u32[]{:S(2)}) copy-start(bf16[2048,640]{1,0:T(8,128)(2,1)} %copy-done.7) | copy-start | bytes 7864324
  682.5 11.1 %copy-start.40 = (f32[192]{0:T(256)S(1)}, f32[192]{0:T(256)}, u32[]{:S(2)}) copy-start(f32[192]{0:T(256)} %copy-done.39) | copy-start | bytes 2308
  693.6 8.9 %copy-start.18 = (bf16[1,2048,192]{1,2,0:T(8,128)(2,1)S(1)}, bf16[1,2048,192]{1,2,0:T(8,128)(2,1)}, u32[]{:S(2)}) copy-start(bf16[1,2048,192]{1,2,0:T(8,128)(2,1)} %stack.24) | copy-start | bytes 2359300
  698.5 13.7 %all-to-all-start.1 = ((bf16[8,192,80]{1,2,0:T(8,128)(2,1)}), bf16[8,192,80]{1,2,0:T(8,128)(2,1)}, u32[]{:S(2)}, u32[]{:S(2)}) async-start(bf16[8,192,80]{1,2,0:T(8,128)(2,1)} %bitcast.136), calls=%async_computation.1 | async-start | bytes 655360 | tf_op jit(solution)/shard_map/all_to_all | solution.py:19
  712.2 56.7 %all-to-all-start = ((bf16[8,3,80,192]{3,2,1,0:T(8,128)(2,1)}), bf16[8,3,80,192]{3,2,1,0:T(8,128)(2,1)}, u32[]{:S(2)}, u32[]{:S(2)}) async-start(bf16[8,3,80,192]{3,2,1,0:T(8,128)(2,1)} %copy.39), calls=%async_computation | async-start | bytes 1966080 | tf_op jit(solution)/shard_map/all_to_all | solution.py:19
  (26 other events, 49.8 us)
Sparse Core Ops, SparseCore 0:
  166.6 104.4 all-reduce.5
  296.2 103.1 all-reduce.7
  423.3 103.1 all-reduce.9
  670.4 104.0 all-reduce.11
where the time goes:
time: 795 us; the launch traced here: 784 us
  waiting for transfers between devices  284 us (36%)
  matrix products  188 us (24%)
  other arithmetic  107 us (13%)
  blocking collectives  89.2 us (11%)
  local copies, waits for them, and re-layouts  77.6 us (10%)
  starting transfers between devices  17.1 us (2%)
  between operations  14.7 us (2%)
    psum x1, waiting for transfers between devices, body(): lax.psum(jnp.dot(act_low, down_full, preferred_element_type=jnp.float32)....  103 us
    psum x1, waiting for transfers between devices, body(): lax.psum(hidden_part.astype(jnp.bfloat16), 'mp').astype(jnp.float32)  90.5 us
    psum x1, waiting for transfers between devices, body(): lax.psum(jnp.dot(mixed_low, out_full, preferred_element_type=jnp.float32)...  81.7 us
    dot_general x8, matrix products, scores_at(): jnp.einsum('qhd,khd->hqk', query_block, keys_all, preferred_element_type=...  54.9 us
    psum x1, blocking collectives, body(): lax.psum((padded_qkv, padded_up, out_bias_term, gain_one_term, shift_one_...  44.5 us
    dynamic_update_slice x12, local copies, waits for them, and re-layouts, body(): attended, all_maxima, all_totals = lax.map(attend, jnp.arange(block_count))  38.5 us
    reduce_sum x4, other arithmetic, attend(): totals = jnp.sum(raised, -1, keepdims=True)  27 us
    dot_general x4, matrix products, attend(): jnp.einsum('hqk,khd->qhd', prob_low, values, preferred_element_type=jnp.f...  26.6 us
  transfers between devices with their start and end apart: 8, of which 5 were waited for; matrix products, arithmetic and copies ran while one was open for 23% of the time, Pallas kernels for 0%

commit v1 on v0

--- a/solution.py
+++ b/solution.py
@@ -220,17 +220,20 @@
         jnp.zeros((mp_size * hidden_cols,), jnp.float32), bias_up, (mp_index * hidden_cols,)
     )
     summed = lax.psum(
-        (
-            padded_qkv,
-            padded_up,
-            out_bias_term,
-            gain_one_term,
-            shift_one_term,
-            down_bias_term,
-            gain_two_term,
-            shift_two_term,
+        lax.psum(
+            (
+                padded_qkv,
+                padded_up,
+                out_bias_term,
+                gain_one_term,
+                shift_one_term,
+                down_bias_term,
+                gain_two_term,
+                shift_two_term,
+            ),
+            "mp",
         ),
-        ("dp", "mp"),
+        "dp",
     )
     qkv_bias_grad = lax.dynamic_slice_in_dim(summed[0], mp_index * slot_width, slot_width, 1)
     up_bias_grad = lax.dynamic_slice_in_dim(summed[1], mp_index * hidden_cols, hidden_cols, 0)

time: 795 us -> 796 us (level)
    psum x1, blocking collectives: 44.5 us -> 18 us  [body(): lax.psum((padded_qkv, padded_up, out_bias_term, gain_one_term, shift_one_...]
    psum x0 -> x1, blocking collectives: none -> 25 us  [body(): lax.psum(lax.psum((padded_qkv, padded_up, out_bias_term, gain_one_term, s...]
where the time goes in v1:
time: 796 us; the launch traced here: 786 us
  waiting for transfers between devices  290 us (36%)
  matrix products  192 us (24%)
  other arithmetic  106 us (13%)
  blocking collectives  87.4 us (11%)
  local copies, waits for them, and re-layouts  74.2 us (9%)
  starting transfers between devices  16.3 us (2%)
  between operations  14.6 us (2%)
    psum x1, waiting for transfers between devices, body(): lax.psum(jnp.dot(act_low, down_full, preferred_element_type=jnp.float32)....  103 us
    psum x1, waiting for transfers between devices, body(): lax.psum(hidden_part.astype(jnp.bfloat16), 'mp').astype(jnp.float32)  90.5 us
    psum x1, waiting for transfers between devices, body(): lax.psum(jnp.dot(mixed_low, out_full, preferred_element_type=jnp.float32)...  81.9 us
    dot_general x8, matrix products, scores_at(): jnp.einsum('qhd,khd->hqk', query_block, keys_all, preferred_element_type=...  58.2 us
    dynamic_update_slice x12, local copies, waits for them, and re-layouts, body(): attended, all_maxima, all_totals = lax.map(attend, jnp.arange(block_count))  38.5 us
    reduce_sum x4, other arithmetic, attend(): totals = jnp.sum(raised, -1, keepdims=True)  26.9 us
    dot_general x4, matrix products, attend(): jnp.einsum('hqk,khd->qhd', prob_low, values, preferred_element_type=jnp.f...  26.5 us
    psum x1, blocking collectives, body(): lax.psum(lax.psum((padded_qkv, padded_up, out_bias_term, gain_one_term, s...  25 us
  transfers between devices with their start and end apart: 8, of which 5 were waited for; matrix products, arithmetic and copies ran while one was open for 23% of the time, Pallas kernels for 0%

profile of v1, /device:TPU:0, one launch (start us, length us, event | category | flops | bytes accessed | tf_op | source)
XLA Modules:
  0.0 785.6 jit_solution(12784784941886100501)
XLA Ops:
  8.2 11.1 %all_gather.13 = bf16[192,640]{0,1:T(8,128)(2,1)S(1)} all-gather(bf16[192,80]{0,1:T(8,128)(2,1)} %param.23), channel_id=1, replica_groups=mesh['dp'=8,'mp'=4] {'dp'}, dimensions={1}, use_global_device_ids=true | all-gather | bytes 276480 | tf_op jit(solution)/shard_map/all_gather | solution.py:62
  19.3 10.8 %all_gather.12 = bf16[3,640,192]{2,1,0:T(8,128)(2,1)S(1)} all-gather(bf16[3,80,192]{2,1,0:T(8,128)(2,1)} %param.21), channel_id=1, replica_groups=mesh['dp'=8,'mp'=4] {'dp'}, dimensions={1}, use_global_device_ids=true | all-gather | bytes 829440 | tf_op jit(solution)/shard_map/all_gather | solution.py:61
  35.8 127.1 %while.29 = (s32[]{:T(128)}, f32[4,512,3,64]{1,0,3,2:T(4,128)}, f32[4,3,512,1]{2,1,3,0:T(4,128)}, f32[4,3,512,1]{2,1,3,0:T(4,128)S(1)}, s32[4]{0:T(128)S(1)}, /*...) while((s32[]{:T(128)}, f32[4,512,3,64]{1,0,3,2:T(4,128)}, ...), condition=%wide.region_3.4_spmd, body=%wide.region_0.3_spmd.sunk | while | flops 844100608 | bytes 45756624 | solution.py:108
  37.8 6.8 fusion.104
  44.6 6.7 fusion.105
  51.3 6.6 fusion.106
  59.0 8.6 %dynamic_update_slice.30 = f32[4,512,3,64]{1,0,3,2:T(4,128)} dynamic-update-slice(f32[4,512,3,64]{1,0,3,2:T(4,128)} %get-tuple-element.421, f32[1,512,3,64]{1,0,3,2:T(1,128)S(1)} %copy.68, s32[]{:T(128)S(6)} %copy.77, s32[]{:T(128)} %constant.76.clone.1..sunk, s32[]{:T(128)} %constant.76.clone.1..sunk, s32[]{:T(128)} %constant.76.clone.1..sunk) | dynamic-update-slice | bytes 786436 | tf_op jit(solution)/shard_map/while/body/jit(dynamic_update_index_in_dim)/dynamic_update_slice | solution.py:108
  69.6 6.8 fusion.104
  76.4 6.7 fusion.105
  83.1 6.6 fusion.106
  90.7 8.6 %dynamic_update_slice.30 = f32[4,512,3,64]{1,0,3,2:T(4,128)} dynamic-update-slice(f32[4,512,3,64]{1,0,3,2:T(4,128)} %get-tuple-element.421, f32[1,512,3,64]{1,0,3,2:T(1,128)S(1)} %copy.68, s32[]{:T(128)S(6)} %copy.77, s32[]{:T(128)} %constant.76.clone.1..sunk, s32[]{:T(128)} %constant.76.clone.1..sunk, s32[]{:T(128)} %constant.76.clone.1..sunk) | dynamic-update-slice | bytes 786436 | tf_op jit(solution)/shard_map/while/body/jit(dynamic_update_index_in_dim)/dynamic_update_slice | solution.py:108
  101.3 6.8 fusion.104
  108.1 6.7 fusion.105
  114.9 6.6 fusion.106
  122.5 8.6 %dynamic_update_slice.30 = f32[4,512,3,64]{1,0,3,2:T(4,128)} dynamic-update-slice(f32[4,512,3,64]{1,0,3,2:T(4,128)} %get-tuple-element.421, f32[1,512,3,64]{1,0,3,2:T(1,128)S(1)} %copy.68, s32[]{:T(128)S(6)} %copy.77, s32[]{:T(128)} %constant.76.clone.1..sunk, s32[]{:T(128)} %constant.76.clone.1..sunk, s32[]{:T(128)} %constant.76.clone.1..sunk) | dynamic-update-slice | bytes 786436 | tf_op jit(solution)/shard_map/while/body/jit(dynamic_update_index_in_dim)/dynamic_update_slice | solution.py:108
  133.1 6.8 fusion.104
  139.9 6.7 fusion.105
  146.7 6.6 fusion.106
  154.3 8.6 %dynamic_update_slice.30 = f32[4,512,3,64]{1,0,3,2:T(4,128)} dynamic-update-slice(f32[4,512,3,64]{1,0,3,2:T(4,128)} %get-tuple-element.421, f32[1,512,3,64]{1,0,3,2:T(1,128)S(1)} %copy.68, s32[]{:T(128)S(6)} %copy.77, s32[]{:T(128)} %constant.76.clone.1..sunk, s32[]{:T(128)} %constant.76.clone.1..sunk, s32[]{:T(128)} %constant.76.clone.1..sunk) | dynamic-update-slice | bytes 786436 | tf_op jit(solution)/shard_map/while/body/jit(dynamic_update_index_in_dim)/dynamic_update_slice | solution.py:108
  168.3 10.6 %all_gather.14 = bf16[640,560]{1,0:T(8,128)(2,1)S(1)} all-gather(bf16[80,560]{1,0:T(8,128)(2,1)} %param.27), channel_id=1, replica_groups=mesh['dp'=8,'mp'=4] {'dp'}, dimensions={0}, use_global_device_ids=true | all-gather | bytes 806400 | tf_op jit(solution)/shard_map/all_gather | solution.py:63
  178.9 12.0 %all_gather.15 = bf16[560,640]{0,1:T(8,128)(2,1)} all-gather(bf16[560,80]{0,1:T(8,128)(2,1)} %param.29), channel_id=1, replica_groups=mesh['dp'=8,'mp'=4] {'dp'}, dimensions={1}, use_global_device_ids=true | all-gather | bytes 806400 | tf_op jit(solution)/shard_map/all_gather | solution.py:64
  190.9 81.9 %all-reduce.7.cloned.1.call-done = bf16[2048,640]{1,0:T(8,128)(2,1)} async-done(((bf16[2048,640]{1,0:T(8,128)(2,1)}), bf16[2048,640]{1,0:T(8,128)(2,1)}) %all-reduce.7.cloned.1.call-update) | async-done | bytes 2621456 | tf_op jit(solution)/shard_map/psum | solution.py:116
  279.6 13.4 %multiply_convert_fusion.1 = (bf16[2048,560]{0,1:T(8,128)(2,1)S(1)}, f32[2048,560]{0,1:T(8,128)}, f32[2048,560]{0,1:T(8,128)}) fusion(f32[560]{0:T(1024)S(1)} %copy-done.39, bf16[640,560]{1,0:T(8,128)(2,1)S(1)} %all_gather.14, f32[2048,640]{1,0:T(8,128)S(1)} %subtract_multiply_fusion.3, f32[640]{0:T(1024)S(1)} %copy-done.31, f32[640]{0:T(1024)S(1)} %copy-done.26), kind=kOutput, calls=%fused_computation.61 | convolution fusion | flops 1547632640 | bytes 17435840 | tf_op jit(solution)/shard_map/dot_general | solution.py:123
  298.7 103.0 %all-reduce.9.cloned.1.call-done = bf16[2048,640]{1,0:T(8,128)(2,1)} async-done(((bf16[2048,640]{1,0:T(8,128)(2,1)}), bf16[2048,640]{1,0:T(8,128)(2,1)}) %all-reduce.9.cloned.1.call-update) | async-done | bytes 2621456 | tf_op jit(solution)/shard_map/psum | solution.py:125
  401.7 4.5 fusion.52
  415.8 4.5 convert_reduce_fusion
  426.2 5.3 convolution_convert_fusion.5
  438.4 90.5 %all-reduce.11.cloned.1.call-done = bf16[2048,640]{1,0:T(8,128)(2,1)} async-done(((bf16[2048,640]{1,0:T(8,128)(2,1)}), bf16[2048,640]{1,0:T(8,128)(2,1)}) %all-reduce.11.cloned.1.call-update) | async-done | bytes 2621456 | tf_op jit(solution)/shard_map/psum | solution.py:144
  528.9 6.9 multiply_reduce_fusion.5
  535.9 6.6 fusion.57
  546.1 115.1 %while.30 = (s32[]{:T(128)}, f32[2048,3,64]{0,2,1:T(8,128)S(1)}, f32[2048,3,64]{0,2,1:T(8,128)S(1)}, bf16[4,512,3,64]{1,3,2,0:T(8,128)(2,1)}, s32[4]{0:T(128)S(1...) while((s32[]{:T(128)}, f32[2048,3,64]{0,2,1:T(8,128)S(1)}, ...), condition=%wide.region_17.18_spmd.clone, body=%wide.region_15.17_spmd.clone.sunk | while | flops 2047834624 | bytes 118950256 | solution.py:184
  552.0 7.8 multiply_reduce_fusion.10
  559.8 5.5 multiply_convert_fusion.6
  565.3 6.2 fusion.118
  580.8 7.8 multiply_reduce_fusion.10
  588.6 5.5 multiply_convert_fusion.6
  594.1 6.2 fusion.118
  609.6 7.8 multiply_reduce_fusion.10
  617.4 5.5 multiply_convert_fusion.6
  622.9 6.2 fusion.118
  638.4 7.8 multiply_reduce_fusion.10
  646.2 5.5 multiply_convert_fusion.6
  651.6 6.2 fusion.118
  672.9 5.1 convolution_convert_fusion.4
  703.9 4.8 fusion.46
  719.5 18.0 %all-reduce.1 = (f32[2,768]{1,0:T(2,128)S(1)}, f32[640]{0:T(1024)S(1)}, f32[640]{0:T(1024)S(1)}, f32[640]{0:T(1024)S(1)}, f32[2240]{0:T(1024)S(1)}, /*index=5*/f...) all-reduce(f32[2,768]{1,0:T(2,128)S(1)} %dynamic_update_slice.20, ...), channel_id=1, replica_groups=mesh['dp'=8,'mp'=4] {'mp'}, use_global_device_ids=true, to_apply=%region_22.23 | all-reduce | flops 7616 | bytes 60928 | tf_op jit(solution)/shard_map/psum | solution.py:223
  737.5 25.0 %all-reduce = (f32[2,768]{1,0:T(2,128)S(1)}, f32[640]{0:T(1024)}, f32[640]{0:T(1024)}, f32[640]{0:T(1024)}, f32[2240]{0:T(1024)S(1)}, /*index=5*/f32[640]{0:T(1024)}, f32[640]{0:T(1024)}, f32[640]{0:T(1024)}) all-reduce(f32[2,768]{1,0:T(2,128)S(1)} %get-tuple-element.230, ...), channel_id=1, replica_groups=mesh['dp'=8,'mp'=4] {'dp'}, use_global_device_ids=true, to_apply=%region_23.24 | all-reduce | flops 7616 | bytes 60928 | tf_op jit(solution)/shard_map/psum | solution.py:222
  765.3 11.1 %all-reduce.13.cloned.1.call-done = bf16[2048,640]{1,0:T(8,128)(2,1)} async-done(((bf16[2048,640]{1,0:T(8,128)(2,1)}), bf16[2048,640]{1,0:T(8,128)(2,1)}) %all-reduce.13.cloned.1.call-update) | async-done | bytes 2621456 | tf_op jit(solution)/shard_map/psum | solution.py:199
  (253 shorter events, 147.3 us)
Async XLA Ops:
  7.2 265.6 %all-reduce.7.cloned.1.call-start = ((), (), s32[]{:S(2)}) async-start(), calls=%async_computation.4 | async-start | bytes 5242880 | tf_op jit(solution)/shard_map/psum | solution.py:116
  7.4 158.1 %copy-start.34 = (f32[192]{0:T(256)}, f32[192]{0:T(256)S(1)}, u32[]{:S(2)}) copy-start(f32[192]{0:T(256)S(1)} %mul.192) | copy-start | bytes 2308
  30.1 4.6 copy-start.20
  162.9 5.3 copy-start.2
  162.9 5.3 copy-start.4
  165.5 110.9 %copy-start.11 = (f32[24,8,4,512]{3,1,2,0:T(8,128)}, f32[24,8,4,512]{3,1,2,0:T(8,128)S(1)}, u32[]{:S(2)}) copy-start(f32[24,8,4,512]{3,1,2,0:T(8,128)S(1)} %copy.66) | copy-start | bytes 4718596
  165.5 107.3 %copy-start.33 = (f32[640]{0:T(1024)S(1)}, f32[640]{0:T(1024)}, u32[]{:S(2)}) copy-start(f32[640]{0:T(1024)} %param.24) | copy-start | bytes 7684
  168.3 233.5 %all-reduce.9.cloned.1.call-start = ((), (), s32[]{:S(2)}) async-start(), calls=%async_computation.5 | async-start | bytes 5242880 | tf_op jit(solution)/shard_map/psum | solution.py:125
  272.8 3.6 copy-start.9
  272.8 4.1 copy-start.10
  279.6 13.4 %copy-start = (f32[2048,640]{1,0:T(8,128)}, f32[2048,640]{1,0:T(8,128)S(1)}, u32[]{:S(2)}) copy-start(f32[2048,640]{1,0:T(8,128)S(1)} %subtract_multiply_fusion.3) | copy-start | bytes 15728644
  279.6 14.8 %copy-start.22 = (bf16[560,640]{0,1:T(8,128)(2,1)S(1)}, bf16[560,640]{0,1:T(8,128)(2,1)}, u32[]{:S(2)}) copy-start(bf16[560,640]{0,1:T(8,128)(2,1)} %all_gather.15) | copy-start | bytes 2150404
  294.4 107.3 %copy-start.30 = (f32[640]{0:T(1024)S(1)}, f32[640]{0:T(1024)}, u32[]{:S(2)}) copy-start(f32[640]{0:T(1024)} %param.30) | copy-start | bytes 7684
  298.5 230.4 %all-reduce.11.cloned.1.call-start = ((), (), s32[]{:S(2)}) async-start(), calls=%async_computation.6 | async-start | bytes 5242880 | tf_op jit(solution)/shard_map/psum | solution.py:144
  401.7 4.6 copy-start.8
  401.7 8.1 %slice-start = ((s8[5242880]{0:T(1024)(128)(4,1)}), s8[1048576]{0:T(1024)(128)(4,1)S(1)}, s32[]{:S(2)}) async-start(s8[5242880]{0:T(1024)(128)(4,1)} %bitcast.122), calls=%async_computation.8 | async-start | bytes 2097152
  406.3 3.6 copy-start.3
  406.3 3.6 copy-start.28
  406.3 4.5 slice-start.1
  406.3 9.4 %slice-start.2 = ((s8[4587520]{0:T(1024)(128)(4,1)}), s8[4194304]{0:T(1024)(128)(4,1)S(1)}, s32[]{:S(2)}) async-start(s8[4587520]{0:T(1024)(128)(4,1)} %bitcast.140), calls=%async_computation.10 | async-start | bytes 8388608
  406.3 9.4 %slice-start.4 = ((s8[4587520]{0:T(1024)(128)(4,1)}), s8[4194304]{0:T(1024)(128)(4,1)S(1)}, s32[]{:S(2)}) async-start(s8[4587520]{0:T(1024)(128)(4,1)} %bitcast.142), calls=%async_computation.12 | async-start | bytes 8388608
  410.9 4.9 slice-start.3
  410.9 4.9 slice-start.5
  415.7 4.6 copy-start.13
  433.7 245.6 %all-to-all-start.3 = ((bf16[8,560,80]{1,2,0:T(8,128)(2,1)}), bf16[8,560,80]{1,2,0:T(8,128)(2,1)}, u32[]{:S(2)}, u32[]{:S(2)}) async-start(bf16[8,560,80]{1,2,0:T(8,128)(2,1)} %bitcast.130), calls=%async_computation.3 | async-start | bytes 1638400 | tf_op jit(solution)/shard_map/all_to_all | solution.py:19
  438.0 338.4 %all-reduce.13.cloned.1.call-start = ((), (), s32[]{:S(2)}) async-start(), calls=%async_computation.7 | async-start | bytes 5242880 | tf_op jit(solution)/shard_map/psum | solution.py:199
  535.9 6.6 copy-start.7
  535.9 9.2 %copy-start.38 = (bf16[3]{0:T(256)(128)(2,1)S(1)}, bf16[3]{0:T(256)(128)(2,1)}, u32[]{:S(2)}) copy-start(bf16[3]{0:T(256)(128)(2,1)} %fusion.55) | copy-start | bytes 22
  548.8 3.2 copy-start.5
  548.8 3.2 copy-start.14
  565.3 6.2 copy-start.23
  594.0 6.2 copy-start.23
  606.4 3.2 copy-start.5
  606.4 3.2 copy-start.14
  622.8 6.2 copy-start.23
  651.6 6.2 copy-start.23
  668.9 4.0 copy-start.27
  668.9 4.0 copy-start.32
  679.3 8.2 %copy-start.37 = (f32[560]{0:T(1024)S(1)}, f32[560]{0:T(1024)}, u32[]{:S(2)}) copy-start(f32[560]{0:T(1024)} %get-tuple-element.238) | copy-start | bytes 6724
  679.3 8.5 %copy-start.29 = (f32[640]{0:T(1024)S(1)}, f32[640]{0:T(1024)}, u32[]{:S(2)}) copy-start(f32[640]{0:T(1024)} %param.31) | copy-start | bytes 7684
  679.3 8.5 %copy-start.36 = (f32[640]{0:T(1024)S(1)}, f32[640]{0:T(1024)}, u32[]{:S(2)}) copy-start(f32[640]{0:T(1024)} %param.32) | copy-start | bytes 7684
  679.3 16.7 %all-to-all-start.2 = ((bf16[8,80,560]{2,1,0:T(8,128)(2,1)}), bf16[8,80,560]{2,1,0:T(8,128)(2,1)S(1)}, u32[]{:S(2)}, u32[]{:S(2)}) async-start(bf16[8,80,560]{2,1,0:T(8,128)(2,1)} %bitcast.21), calls=%async_computation.2 | async-start | bytes 1638400 | tf_op jit(solution)/shard_map/all_to_all | solution.py:19
  687.5 9.4 %copy-start.12 = (f32[24,8,4,512]{3,1,2,0:T(8,128)S(1)}, f32[24,8,4,512]{3,1,2,0:T(8,128)}, u32[]{:S(2)}) copy-start(f32[24,8,4,512]{3,1,2,0:T(8,128)} %copy-done.11) | copy-start | bytes 4718596
  687.5 9.4 %copy-start.35 = (f32[192]{0:T(256)S(1)}, f32[192]{0:T(256)}, u32[]{:S(2)}) copy-start(f32[192]{0:T(256)} %copy-done.34) | copy-start | bytes 2308
  690.8 13.1 %copy-start.16 = (bf16[1,2048,192]{1,2,0:T(8,128)(2,1)S(1)}, bf16[1,2048,192]{1,2,0:T(8,128)(2,1)}, u32[]{:S(2)}) copy-start(bf16[1,2048,192]{1,2,0:T(8,128)(2,1)} %stack.24) | copy-start | bytes 2359300
  696.9 7.0 copy-start.18
  700.4 11.0 %all-to-all-start.1 = ((bf16[8,192,80]{1,2,0:T(8,128)(2,1)}), bf16[8,192,80]{1,2,0:T(8,128)(2,1)S(1)}, u32[]{:S(2)}, u32[]{:S(2)}) async-start(bf16[8,192,80]{1,2,0:T(8,128)(2,1)} %bitcast.20), calls=%async_computation.1 | async-start | bytes 655360 | tf_op jit(solution)/shard_map/all_to_all | solution.py:19
  711.4 53.0 %all-to-all-start = ((bf16[8,3,80,192]{3,2,1,0:T(8,128)(2,1)}), bf16[8,3,80,192]{3,2,1,0:T(8,128)(2,1)S(1)}, u32[]{:S(2)}, u32[]{:S(2)}) async-start(bf16[8,3,80,192]{3,2,1,0:T(8,128)(2,1)} %copy.39), calls=%async_computation | async-start | bytes 1966080 | tf_op jit(solution)/shard_map/all_to_all | solution.py:19
  (20 other events, 35.1 us)
Sparse Core Ops, SparseCore 0:
  168.4 104.4 all-reduce.6
  298.6 103.1 all-reduce.8
  425.8 103.1 all-reduce.10
  673.0 103.3 all-reduce.12
